TPU v7x, 32 devices: a whole 2x2x4 slice. The times are simulated.
32 devices in a mesh: plane: 4 (over y, core), frame: 8 (over z, x).
Axes of the slice: x: 2, y: 2, z: 4, core: 2. Of those that a mesh axis runs over, the one named last changes fastest.
Arguments:
- image: float32 [8, 8, 2, 128, 128], P('plane', 'frame'), may hold values from -6 to 6
- sens: bfloat16 [4, 8, 2, 128, 128], P(None, 'plane'), may hold values from -3 to 3
- kspace: bfloat16 [4, 8, 8, 2, 128, 128], P(None, 'plane', 'frame'), may hold values from -6 to 6
- offsets: int32 [8, 128], P('frame'), may hold values from 0 to 3
- shifts: int32 [2], replicated, may hold values from 0 to 7
- step_size: float32 [1], replicated, may hold values from 0.5 to 1.5
- threshold: float32 [1], replicated, may hold values from 100 to 1000
Outputs:
- new_image: float32 [8, 8, 2, 128, 128], P('plane', 'frame')
All inputs are finite; a program needn't handle non-finite values.
Results may differ from a plain program's by a relative error of at most 0.0003.
Values sent between devices are 32-bit elements; how exact they have to be, the bound alone decides.
A program may use at most 64 MiB of HBM per device.

v0:
```python
import math
import jax
import jax.numpy as jnp
from jax import lax
from jax.sharding import PartitionSpec as P

PATCH_Y = 8
PATCH_Z = 8
ACCEL = 4
CENTER = 8


def from_partner(block, axis, distance):
    count = lax.axis_size(axis)
    route = []
    for low in range(count):
        high = low | 1 << distance
        if high != low and high < count:
            route += [(low, high), (high, low)]
    return lax.ppermute(block, axis, route)


def dft_tables(length):
    indices = jnp.arange(length, dtype=jnp.int32)
    phases = indices[:, None] * indices[None, :] % length
    angles = phases.astype(jnp.float32) * (2.0 * math.pi / length)
    norm_scale = 1.0 / math.sqrt(length)
    return (jnp.cos(angles) * norm_scale, jnp.sin(angles) * norm_scale)


def along_z(stacked, right_table, sign, width_z):
    product = jnp.einsum(
        "...z,zw->...w",
        stacked,
        right_table,
        precision=lax.Precision.HIGHEST,
        preferred_element_type=jnp.float32,
    )
    cos_part = product[..., :width_z]
    sin_part = product[..., width_z:]
    real_part = cos_part[..., 0, :, :] + sign * sin_part[..., 1, :, :]
    imag_part = cos_part[..., 1, :, :] - sign * sin_part[..., 0, :, :]
    return jnp.stack([real_part, imag_part], axis=-3)


def along_y(stacked, left_table):
    shape_in = stacked.shape
    merged = stacked.reshape(shape_in[:-3] + (2 * shape_in[-2], shape_in[-1]))
    result = jnp.einsum(
        "ur,...rz->...uz",
        left_table,
        merged,
        precision=lax.Precision.HIGHEST,
        preferred_element_type=jnp.float32,
    )
    return result.reshape(shape_in)


def rotate(casorati):
    frames2, voxels = (casorati.shape[-2], casorati.shape[-1])
    split_parts = casorati.reshape(casorati.shape[:-2] + (frames2 // 2, 2, voxels))
    turned = jnp.stack([-split_parts[..., 1, :], split_parts[..., 0, :]], axis=-2)
    return turned.reshape(casorati.shape)


def gram_of(casorati):
    twin = rotate(casorati)
    first = jnp.einsum(
        "kav,kbv->kab",
        casorati,
        casorati,
        precision=lax.Precision.HIGHEST,
        preferred_element_type=jnp.float32,
    )
    second = jnp.einsum(
        "kav,kbv->kab",
        twin,
        twin,
        precision=lax.Precision.HIGHEST,
        preferred_element_type=jnp.float32,
    )
    return first + second


def shrink(casorati, gram, level):
    order = gram.shape[-1]
    system = gram + level * jnp.eye(order, dtype=jnp.float32)
    factor = jnp.linalg.cholesky(system)
    forward_part = jax.scipy.linalg.solve_triangular(factor, casorati, lower=True)
    solved = jax.scipy.linalg.solve_triangular(factor, forward_part, lower=True, trans=1)
    return casorati - level * solved


def local(image, sens, kspace, offsets, shifts, step_size, threshold):
    planes, frames_dev, _, width_y, width_z = image.shape
    frames = frames_dev * lax.axis_size("frame")
    cos_y, sin_y = dft_tables(width_y)
    cos_z, sin_z = dft_tables(width_z)
    right_table = jnp.concatenate([cos_z, sin_z], axis=1)
    left_forward = jnp.concatenate(
        [jnp.concatenate([cos_y, sin_y], axis=1), jnp.concatenate([-sin_y, cos_y], axis=1)], axis=0
    )
    left_inverse = jnp.concatenate(
        [jnp.concatenate([cos_y, -sin_y], axis=1), jnp.concatenate([sin_y, cos_y], axis=1)], axis=0
    )
    rows_y = jnp.arange(width_y, dtype=jnp.int32)
    rows_z = jnp.arange(width_z, dtype=jnp.int32)
    low_y = (rows_y < CENTER) | (rows_y >= width_y - CENTER)
    low_z = (rows_z < CENTER) | (rows_z >= width_z - CENTER)
    regular = (rows_z[None, None, :] + offsets[:, :, None]) % ACCEL == 0
    sampled = (regular | low_y[None, :, None] & low_z[None, None, :]).astype(jnp.float32)
    image_re = image[:, :, 0]
    image_im = image[:, :, 1]
    maps = sens.astype(jnp.float32)
    sens_re = maps[:, :, 0][:, :, None]
    sens_im = maps[:, :, 1][:, :, None]
    coil_re = sens_re * image_re[None] - sens_im * image_im[None]
    coil_im = sens_re * image_im[None] + sens_im * image_re[None]
    stacked = jnp.stack([coil_re, coil_im], axis=3)
    spectra = along_y(along_z(stacked, right_table, 1.0, width_z), left_forward)
    resid = sampled[None, None, :, None] * (spectra - kspace.astype(jnp.float32))
    returned = along_z(along_y(resid, left_inverse), right_table, -1.0, width_z)
    back_re = returned[:, :, :, 0]
    back_im = returned[:, :, :, 1]
    grad_re = jnp.sum(sens_re * back_re + sens_im * back_im, axis=0)
    grad_im = jnp.sum(sens_re * back_im - sens_im * back_re, axis=0)
    moved = image - step_size[0] * jnp.stack([grad_re, grad_im], axis=2)
    rolled = jnp.roll(moved, (shifts[0], shifts[1]), axis=(3, 4))
    nyb = width_y // PATCH_Y
    nzb = width_z // PATCH_Z
    voxels = planes * PATCH_Y * PATCH_Z
    blocks = rolled.reshape(planes, frames_dev, 2, nyb, PATCH_Y, nzb, PATCH_Z)
    blocks = blocks.transpose(3, 5, 1, 2, 0, 4, 6).reshape(nyb * nzb, frames_dev, 2, voxels)
    regrouped = lax.all_to_all(blocks, "frame", split_axis=0, concat_axis=1, tiled=True)
    count = regrouped.shape[0]
    casorati = regrouped.reshape(count, 2 * frames, voxels)
    level = threshold[0]
    parity = lax.axis_index("plane") % 2
    halfway = count // 2
    first_part = casorati[:halfway]
    second_part = casorati[halfway:]
    kept_part = jnp.where(parity == 0, first_part, second_part)
    outgoing = jnp.where(parity == 0, second_part, first_part)
    incoming = from_partner(outgoing, "plane", 0)
    complete = jnp.concatenate([kept_part, incoming], axis=2)
    finished = shrink(complete, gram_of(complete), level)
    own_part = finished[:, :, :voxels]
    returned_part = from_partner(finished[:, :, voxels:], "plane", 0)
    shrunk = jnp.where(
        parity == 0,
        jnp.concatenate([own_part, returned_part], axis=0),
        jnp.concatenate([returned_part, own_part], axis=0),
    )
    restored = lax.all_to_all(
        shrunk.reshape(count, frames, 2, voxels), "frame", split_axis=1, concat_axis=0, tiled=True
    )
    placed = restored.reshape(nyb, nzb, frames_dev, 2, planes, PATCH_Y, PATCH_Z)
    placed = placed.transpose(4, 2, 3, 0, 5, 1, 6).reshape(planes, frames_dev, 2, width_y, width_z)
    return jnp.roll(placed, (-shifts[0], -shifts[1]), axis=(3, 4))


def solution(mesh):
    in_specs = (
        P("plane", "frame", None, None, None),
        P(None, "plane", None, None, None),
        P(None, "plane", "frame", None, None, None),
        P("frame", None),
        P(),
        P(),
        P(),
    )
    out_specs = P("plane", "frame", None, None, None)
    return jax.shard_map(local, mesh=mesh, in_specs=in_specs, out_specs=out_specs, check_vma=False)
```

profile of v0, /device:TPU:0, one launch (start us, length us, event | category | flops | bytes accessed | tf_op | source)
XLA Modules:
  0.0 114.0 jit_solution(13654522863200061980)
XLA Ops:
  0.0 1.3 %fusion.51 = (s32[1]{0:T(128)}, s32[1]{0:T(128)}) fusion(s32[2]{0:T(128)} %param.13), kind=kLoop, calls=%fused_computation.107 | loop fusion | bytes 16 | tf_op jit(solution)/shard_map/jit(_roll_dynamic)/unstack | solution.py:128
  5.6 1.1 copy_convert_fusion
  6.8 1.0 slice_bitcast_fusion.1
  7.9 1.8 %convolution_bitcast_fusion.1 = f32[4,2,1,2,128,256]{5,4,3,1,0,2:T(8,128)S(1)} fusion(f32[4,2,1,1,128,128]{5,4,3,1,0,2:T(8,128)S(1)} %get-tuple-element.11, f32[4,2,1,1,128,128]{5,4,3,1,0,2:T(8,128)S(1)} %get-tuple-element.10, f32[128,128]{1,0:T(8,128)S(1)} %get-tuple-element.24, f32[128,128]{1,0:T(8,128)S(1)} %get-tuple-element.25), kind=kOutput, calls=%fused_computation.1 | convolution fusion | flops 805601280 | bytes 3276800 | tf_op jit(solution)/shard_map/...z,zw->...w/dot_general | solution.py:32
  9.9 1.8 %convolution_bitcast_fusion.3 = f32[4,2,1,256,128]{3,4,1,0,2:T(8,128)S(1)} fusion(f32[4,2,256,128]{3,2,1,0:T(8,128)S(1)} %bitcast.121, f32[128,128]{1,0:T(8,128)S(1)} %get-tuple-element.25, f32[128,128]{1,0:T(8,128)S(1)} %fusion.44, f32[128,128]{1,0:T(8,128)S(1)} %get-tuple-element.24), kind=kOutput, calls=%fused_computation.3 | convolution fusion | flops 805502976 | bytes 2293760 | tf_op jit(solution)/shard_map/ur,...rz->...uz/dot_general | solution.py:49
  12.2 1.2 %subtract_multiply_fusion = f32[4,2,1,2,128,128]{5,4,3,2,1,0:T(8,128)S(1)} fusion(f32[4,2,1,2,128,128]{5,4,3,2,1,0:T(8,128)S(1)} %bitcast.122, bf16[4,2,1,2,128,128]{5,4,3,2,1,0:T(8,128)(2,1)} %param.11, f32[128,128]{1,0:T(8,128)S(1)} %fusion.43), kind=kLoop, calls=%fused_computation.12 | loop fusion | flops 786432 | bytes 2686976 | tf_op jit(solution)/shard_map/mul | solution.py:121
  13.4 1.8 %convolution_bitcast_fusion.2 = f32[4,2,1,256,128]{3,4,1,0,2:T(8,128)S(1)} fusion(f32[4,2,256,128]{3,2,1,0:T(8,128)S(1)} %bitcast.123, f32[128,128]{1,0:T(8,128)S(1)} %get-tuple-element.25, f32[128,128]{1,0:T(8,128)S(1)} %get-tuple-element.24, f32[128,128]{1,0:T(8,128)S(1)} %fusion.44), kind=kOutput, calls=%fused_computation.2 | convolution fusion | flops 805502976 | bytes 2293760 | tf_op jit(solution)/shard_map/ur,...rz->...uz/dot_general | solution.py:49
  15.5 1.8 %convolution_bitcast_fusion = f32[4,2,1,2,128,256]{5,4,1,0,3,2:T(8,128)S(1)} fusion(f32[4,2,2,128,128]{4,3,2,1,0:T(8,128)S(1)} %bitcast.120, f32[128,128]{1,0:T(8,128)S(1)} %get-tuple-element.24, f32[128,128]{1,0:T(8,128)S(1)} %get-tuple-element.25), kind=kOutput, calls=%fused_computation | convolution fusion | flops 805339136 | bytes 3276800 | tf_op jit(solution)/shard_map/...z,zw->...w/dot_general | solution.py:32
  18.7 3.6 %reshape.304 = f32[2,1,2,16,8,16,8]{6,5,4,3,2,0,1:T(8,128)} reshape(f32[2,1,2,128,128]{4,3,2,1,0:T(8,128)S(1)} %fusion.17) | data formatting | bytes 524288 | tf_op jit(solution)/shard_map/reshape | solution.py:132
  22.3 2.9 %copy.73 = f32[16,16,1,2,2,8,8]{1,0,6,5,4,3,2:T(8,128)S(1)} copy(f32[16,16,1,2,2,8,8]{6,1,5,0,3,4,2:T(8,128)} %bitcast.118) | data formatting | bytes 524288 | tf_op jit(solution)/shard_map/transpose | solution.py:133
  25.2 0.9 reshape.305
  26.1 0.8 copy.74
  27.0 7.3 %all-to-all-start = ((f32[256,1,2,128]{3,2,1,0:T(2,128)}), f32[256,1,2,128]{3,2,1,0:T(2,128)S(1)}, u32[]{:S(2)}, u32[]{:S(2)}) async-start(f32[256,1,2,128]{3,2,1,0:T(2,128)} %copy.74), calls=%async_computation | async-start | bytes 524288 | tf_op jit(solution)/shard_map/all_to_all | solution.py:134
  34.9 8.2 %all-to-all-done = f32[256,1,2,128]{3,2,1,0:T(2,128)S(1)} async-done(((f32[256,1,2,128]{3,2,1,0:T(2,128)}), f32[256,1,2,128]{3,2,1,0:T(2,128)S(1)}, u32[]{:S(2)}, u32[]{:S(2)}) %all-to-all-start) | async-done | bytes 262176 | tf_op jit(solution)/shard_map/all_to_all | solution.py:134
  43.6 1.1 collective-permute-done
  46.4 23.5 %custom-call.11 = f32[16,16,16]{2,1,0:T(8,128)S(1)} custom-call(f32[16,16,16]{2,1,0:T(8,128)S(1)} %fusion.30), custom_call_target="Cholesky" | custom-call | tf_op jit(solution)/shard_map/jit(cholesky)/cholesky | solution.py:88
  70.2 19.8 %custom-call.12 = f32[16,1,16,16]{2,3,1,0:T(8,128)S(1)} custom-call(f32[16,1,16,16]{3,2,1,0:T(8,128)S(1)} %select_bitcast_fusion), custom_call_target="InvertDiagBlocksLowerTriangular" | custom-call | tf_op jit(solution)/shard_map/jit(_solve_triangular)/vmap()/triangular_solve | solution.py:90
  91.1 1.2 %collective-permute-done.1 = f32[16,16,128]{2,1,0:T(8,128)S(1)} collective-permute-done((f32[16,16,128]{2,1,0:T(8,128)S(1)}, f32[16,16,128]{2,1,0:T(8,128)S(1)}, u32[]{:S(2)}, u32[]{:S(2)}) %collective-permute-start.1) | collective-permute-done | bytes 131104 | tf_op jit(solution)/shard_map/ppermute | solution.py:20
  92.3 0.7 maximum_select_fusion
  93.0 3.6 %all-to-all-start.1 = ((f32[32,8,2,128]{3,0,2,1:T(8,128)}), f32[32,8,2,128]{3,0,2,1:T(8,128)S(1)}, u32[]{:S(2)}, u32[]{:S(2)}) async-start(f32[32,8,2,128]{3,0,2,1:T(8,128)} %maximum_select_fusion), calls=%async_computation.1 | async-start | bytes 524288 | tf_op jit(solution)/shard_map/all_to_all | solution.py:154
  97.9 8.0 %all-to-all-done.1 = f32[32,8,2,128]{3,0,2,1:T(8,128)S(1)} async-done(((f32[32,8,2,128]{3,0,2,1:T(8,128)}), f32[32,8,2,128]{3,0,2,1:T(8,128)S(1)}, u32[]{:S(2)}, u32[]{:S(2)}) %all-to-all-start.1) | async-done | bytes 262176 | tf_op jit(solution)/shard_map/all_to_all | solution.py:154
  106.6 2.8 %copy.88 = f32[2,1,2,16,8,16,8]{6,5,4,3,2,0,1:T(8,128)} copy(f32[2,1,2,16,8,16,8]{5,3,6,4,0,2,1:T(8,128)S(1)} %bitcast.119) | data formatting | bytes 524288 | tf_op jit(solution)/shard_map/transpose | solution.py:158
  109.4 3.6 %reshape.309 = f32[2,1,2,128,128]{4,3,2,0,1:T(8,128)S(1)} reshape(f32[2,1,2,16,8,16,8]{6,5,4,3,2,0,1:T(8,128)} %copy.88) | data formatting | bytes 524288 | tf_op jit(solution)/shard_map/reshape | solution.py:158
  113.1 0.9 fusion.15
  (47 shorter events, 6.5 us)
Async XLA Ops:
  9.9 2.2 %copy-start.1 = (s32[1,128]{1,0:T(1,128)S(1)}, s32[1,128]{1,0:T(1,128)}, u32[]{:S(2)}) copy-start(s32[1,128]{1,0:T(1,128)} %param.12) | copy-start | bytes 1540
  17.4 1.0 copy-start
  27.0 16.2 %all-to-all-start = ((f32[256,1,2,128]{3,2,1,0:T(2,128)}), f32[256,1,2,128]{3,2,1,0:T(2,128)S(1)}, u32[]{:S(2)}, u32[]{:S(2)}) async-start(f32[256,1,2,128]{3,2,1,0:T(2,128)} %copy.74), calls=%async_computation | async-start | bytes 524288 | tf_op jit(solution)/shard_map/all_to_all | solution.py:134
  43.3 1.4 %collective-permute-start = (f32[16,16,128]{2,1,0:T(8,128)S(1)}, f32[16,16,128]{2,1,0:T(8,128)S(1)}, u32[]{:S(2)}, u32[]{:S(2)}) collective-permute-start(f32[16,16,128]{2,1,0:T(8,128)S(1)} %bitcast.133), channel_id=1, source_target_pairs={{0,8},{8,0},{16,24},{24,16},{1,9},{9,1},{17,25},{25,17},{2,10},{10... | collective-permute-start | bytes 393224 | tf_op jit(solution)/shard_map/ppermute | solution.py:20
  90.8 1.4 %collective-permute-start.1 = (f32[16,16,128]{2,1,0:T(8,128)S(1)}, f32[16,16,128]{2,1,0:T(8,128)S(1)}, u32[]{:S(2)}, u32[]{:S(2)}) collective-permute-start(f32[16,16,128]{2,1,0:T(8,128)S(1)} %get-tuple-element.13), channel_id=1, source_target_pairs={{0,8},{8,0},{16,24},{24,16},{1,9},{9,1},{17,25},{25,17},{2,10},{10... | collective-permute-start | bytes 393224 | tf_op jit(solution)/shard_map/ppermute | solution.py:20
  93.0 12.9 %all-to-all-start.1 = ((f32[32,8,2,128]{3,0,2,1:T(8,128)}), f32[32,8,2,128]{3,0,2,1:T(8,128)S(1)}, u32[]{:S(2)}, u32[]{:S(2)}) async-start(f32[32,8,2,128]{3,0,2,1:T(8,128)} %maximum_select_fusion), calls=%async_computation.1 | async-start | bytes 524288 | tf_op jit(solution)/shard_map/all_to_all | solution.py:154
where the time goes:
time: 115 us; the launch traced here: 114 us
  other arithmetic  49.6 us (43%)
  local copies, waits for them, and re-layouts  19.3 us (17%)
  waiting for transfers between devices  18.5 us (16%)
  starting transfers between devices  11.2 us (10%)
  matrix products  8.81 us (8%)
  between operations  6.67 us (6%)
    another operation x4, other arithmetic, shrink(): factor = jnp.linalg.cholesky(system)  23.6 us
    another operation x3, other arithmetic, shrink(): jax.scipy.linalg.solve_triangular(factor, forward_part, lower=True, trans=1)  19.9 us
    all_to_all x1, waiting for transfers between devices, local(): lax.all_to_all(blocks, 'frame', split_axis=0, concat_axis=1, tiled=True)  8.25 us
    all_to_all x1, waiting for transfers between devices, local(): lax.all_to_all(shrunk.reshape(count, frames, 2, voxels), 'frame', split_a...  8.01 us
    all_to_all x1, starting transfers between devices, local(): lax.all_to_all(blocks, 'frame', split_axis=0, concat_axis=1, tiled=True)  7.29 us
    reshape x1, local copies, waits for them, and re-layouts, local(): placed.transpose(4, 2, 3, 0, 5, 1, 6)  3.64 us
    dot_general x2, matrix products, along_y(): jnp.einsum('ur,...rz->...uz', left_table, merged, precision=lax.Precision...  3.62 us
    reshape x1, local copies, waits for them, and re-layouts, local(): blocks = rolled.reshape(planes, frames_dev, 2, nyb, PATCH_Y, nzb, PATCH_Z)  3.62 us
  transfers between devices with their start and end apart: 4, of which 4 were waited for; matrix products, arithmetic and copies ran while one was open for 0% of the time, Pallas kernels for 0%

commit v1 on v0

--- a/solution.py
+++ b/solution.py
@@ -151,9 +151,10 @@
         jnp.concatenate([own_part, returned_part], axis=0),
         jnp.concatenate([returned_part, own_part], axis=0),
     )
-    restored = lax.all_to_all(
-        shrunk.reshape(count, frames, 2, voxels), "frame", split_axis=1, concat_axis=0, tiled=True
-    )
+    part = shrunk.reshape(count, frames, 2, voxels)
+    shards = jnp.split(part, lax.axis_size("frame"), axis=1)
+    received = lax.all_to_all(jnp.stack(shards), "frame", 0, 0)
+    restored = jnp.concatenate(received, axis=0)
     placed = restored.reshape(nyb, nzb, frames_dev, 2, planes, PATCH_Y, PATCH_Z)
     placed = placed.transpose(4, 2, 3, 0, 5, 1, 6).reshape(planes, frames_dev, 2, width_y, width_z)
     return jnp.roll(placed, (-shifts[0], -shifts[1]), axis=(3, 4))

time: 115 us -> 119 us (1.035)
  local copies, waits for them, and re-layouts: 19.3 us -> 24.3 us
    unnamed x4 -> x11, local copies, waits for them, and re-layouts: 0.02 us -> 4.34 us
where the time goes in v1:
time: 119 us; the launch traced here: 118 us
  other arithmetic  48.9 us (41%)
  local copies, waits for them, and re-layouts  24.3 us (20%)
  waiting for transfers between devices  18.6 us (16%)
  starting transfers between devices  11.2 us (9%)
  matrix products  8.81 us (7%)
  between operations  6.5 us (5%)
    another operation x4, other arithmetic, shrink(): factor = jnp.linalg.cholesky(system)  23.6 us
    another operation x3, other arithmetic, shrink(): jax.scipy.linalg.solve_triangular(factor, forward_part, lower=True, trans=1)  19.9 us
    all_to_all x1, waiting for transfers between devices, local(): lax.all_to_all(blocks, 'frame', split_axis=0, concat_axis=1, tiled=True)  8.25 us
    all_to_all x1, waiting for transfers between devices, local(): received = lax.all_to_all(jnp.stack(shards), 'frame', 0, 0)  8.05 us
    all_to_all x1, starting transfers between devices, local(): lax.all_to_all(blocks, 'frame', split_axis=0, concat_axis=1, tiled=True)  7.28 us
    unnamed x11, local copies, waits for them, and re-layouts  4.34 us
    reshape x1, local copies, waits for them, and re-layouts, local(): placed.transpose(4, 2, 3, 0, 5, 1, 6)  3.64 us
    dot_general x2, matrix products, along_y(): jnp.einsum('ur,...rz->...uz', left_table, merged, precision=lax.Precision...  3.62 us
  transfers between devices with their start and end apart: 4, of which 4 were waited for; matrix products, arithmetic and copies ran while one was open for 0% of the time, Pallas kernels for 0%

profile of v1, /device:TPU:0, one launch (start us, length us, event | category | flops | bytes accessed | tf_op | source)
XLA Modules:
  0.0 118.3 jit_solution(6855452954320251593)
XLA Ops:
  0.0 1.3 %fusion.52 = (s32[1]{0:T(128)}, s32[1]{0:T(128)}) fusion(s32[2]{0:T(128)} %param.13), kind=kLoop, calls=%fused_computation.116 | loop fusion | bytes 16 | tf_op jit(solution)/shard_map/jit(_roll_dynamic)/unstack | solution.py:128
  5.5 1.1 copy_convert_fusion
  6.6 1.0 slice_bitcast_fusion.1
  7.7 1.8 %convolution_bitcast_fusion.1 = f32[4,2,1,2,128,256]{5,4,3,1,0,2:T(8,128)S(1)} fusion(f32[4,2,1,1,128,128]{5,4,3,1,0,2:T(8,128)S(1)} %get-tuple-element.11, f32[4,2,1,1,128,128]{5,4,3,1,0,2:T(8,128)S(1)} %get-tuple-element.10, f32[128,128]{1,0:T(8,128)S(1)} %get-tuple-element.32, f32[128,128]{1,0:T(8,128)S(1)} %get-tuple-element.33), kind=kOutput, calls=%fused_computation.1 | convolution fusion | flops 805601280 | bytes 3276800 | tf_op jit(solution)/shard_map/...z,zw->...w/dot_general | solution.py:32
  9.7 1.8 %convolution_bitcast_fusion.3 = f32[4,2,1,256,128]{3,4,1,0,2:T(8,128)S(1)} fusion(f32[4,2,256,128]{3,2,1,0:T(8,128)S(1)} %bitcast.126, f32[128,128]{1,0:T(8,128)S(1)} %get-tuple-element.33, f32[128,128]{1,0:T(8,128)S(1)} %fusion.44, f32[128,128]{1,0:T(8,128)S(1)} %get-tuple-element.32), kind=kOutput, calls=%fused_computation.3 | convolution fusion | flops 805502976 | bytes 2293760 | tf_op jit(solution)/shard_map/ur,...rz->...uz/dot_general | solution.py:49
  12.0 1.2 subtract_multiply_fusion
  13.2 1.8 %convolution_bitcast_fusion.2 = f32[4,2,1,256,128]{3,4,1,0,2:T(8,128)S(1)} fusion(f32[4,2,256,128]{3,2,1,0:T(8,128)S(1)} %bitcast.128, f32[128,128]{1,0:T(8,128)S(1)} %get-tuple-element.33, f32[128,128]{1,0:T(8,128)S(1)} %get-tuple-element.32, f32[128,128]{1,0:T(8,128)S(1)} %fusion.44), kind=kOutput, calls=%fused_computation.2 | convolution fusion | flops 805502976 | bytes 2293760 | tf_op jit(solution)/shard_map/ur,...rz->...uz/dot_general | solution.py:49
  15.4 1.8 %convolution_bitcast_fusion = f32[4,2,1,2,128,256]{5,4,1,0,3,2:T(8,128)S(1)} fusion(f32[4,2,2,128,128]{4,3,2,1,0:T(8,128)S(1)} %bitcast.125, f32[128,128]{1,0:T(8,128)S(1)} %get-tuple-element.32, f32[128,128]{1,0:T(8,128)S(1)} %get-tuple-element.33), kind=kOutput, calls=%fused_computation | convolution fusion | flops 805339136 | bytes 3276800 | tf_op jit(solution)/shard_map/...z,zw->...w/dot_general | solution.py:32
  18.5 3.6 %reshape.300 = f32[2,1,2,16,8,16,8]{6,5,4,3,2,0,1:T(8,128)} reshape(f32[2,1,2,128,128]{4,3,2,1,0:T(8,128)S(1)} %fusion.17) | data formatting | bytes 524288 | tf_op jit(solution)/shard_map/reshape | solution.py:132
  22.1 2.9 %copy.94 = f32[16,16,1,2,2,8,8]{1,0,6,5,4,3,2:T(8,128)S(1)} copy(f32[16,16,1,2,2,8,8]{6,1,5,0,3,4,2:T(8,128)} %bitcast.123) | data formatting | bytes 524288 | tf_op jit(solution)/shard_map/transpose | solution.py:133
  25.0 0.9 reshape.301
  26.0 0.8 copy.95
  26.8 7.3 %all-to-all-start = ((f32[256,1,2,128]{3,2,1,0:T(2,128)}), f32[256,1,2,128]{3,2,1,0:T(2,128)S(1)}, u32[]{:S(2)}, u32[]{:S(2)}) async-start(f32[256,1,2,128]{3,2,1,0:T(2,128)} %copy.95), calls=%async_computation | async-start | bytes 524288 | tf_op jit(solution)/shard_map/all_to_all | solution.py:134
  34.7 8.3 %all-to-all-done = f32[256,1,2,128]{3,2,1,0:T(2,128)S(1)} async-done(((f32[256,1,2,128]{3,2,1,0:T(2,128)}), f32[256,1,2,128]{3,2,1,0:T(2,128)S(1)}, u32[]{:S(2)}, u32[]{:S(2)}) %all-to-all-start) | async-done | bytes 262176 | tf_op jit(solution)/shard_map/all_to_all | solution.py:134
  43.4 1.1 collective-permute-done
  46.3 23.5 %custom-call.11 = f32[16,16,16]{2,1,0:T(8,128)S(1)} custom-call(f32[16,16,16]{2,1,0:T(8,128)S(1)} %fusion.30), custom_call_target="Cholesky" | custom-call | tf_op jit(solution)/shard_map/jit(cholesky)/cholesky | solution.py:88
  70.0 19.8 %custom-call.12 = f32[16,1,16,16]{2,3,1,0:T(8,128)S(1)} custom-call(f32[16,1,16,16]{3,2,1,0:T(8,128)S(1)} %select_bitcast_fusion), custom_call_target="InvertDiagBlocksLowerTriangular" | custom-call | tf_op jit(solution)/shard_map/jit(_solve_triangular)/vmap()/triangular_solve | solution.py:90
  90.9 1.2 %collective-permute-done.1 = f32[16,16,128]{2,1,0:T(8,128)S(1)} collective-permute-done((f32[16,16,128]{2,1,0:T(8,128)S(1)}, f32[16,16,128]{2,1,0:T(8,128)S(1)}, u32[]{:S(2)}, u32[]{:S(2)}) %collective-permute-start.1) | collective-permute-done | bytes 131104 | tf_op jit(solution)/shard_map/ppermute | solution.py:20
  92.3 0.6 copy_dynamic-update-slice_fusion.7
  97.2 3.6 %all-to-all-start.1 = ((f32[8,32,1,2,128]{4,1,3,2,0:T(8,128)}), f32[8,32,1,2,128]{4,1,3,2,0:T(8,128)S(1)}, u32[]{:S(2)}, u32[]{:S(2)}) async-start(f32[8,32,1,2,128]{4,1,3,2,0:T(8,128)} %copy_dynamic-update-slice_fusion), calls=%async_computation.1 | async-start | bytes 524288 | tf_op jit(solution)/shard_map/all_to_all | solution.py:156
  102.1 8.1 %all-to-all-done.1 = f32[8,32,1,2,128]{4,1,3,2,0:T(8,128)S(1)} async-done(((f32[8,32,1,2,128]{4,1,3,2,0:T(8,128)}), f32[8,32,1,2,128]{4,1,3,2,0:T(8,128)S(1)}, u32[]{:S(2)}, u32[]{:S(2)}) %all-to-all-start.1) | async-done | bytes 262176 | tf_op jit(solution)/shard_map/all_to_all | solution.py:156
  110.8 2.8 %copy.117 = f32[2,1,2,16,8,16,8]{6,5,4,3,2,0,1:T(8,128)} copy(f32[2,1,2,16,8,16,8]{5,3,6,4,0,2,1:T(8,128)S(1)} %bitcast.124) | data formatting | bytes 524288 | tf_op jit(solution)/shard_map/transpose | solution.py:159
  113.6 3.6 %reshape.304 = f32[2,1,2,128,128]{4,3,2,0,1:T(8,128)S(1)} reshape(f32[2,1,2,16,8,16,8]{6,5,4,3,2,0,1:T(8,128)} %copy.117) | data formatting | bytes 524288 | tf_op jit(solution)/shard_map/reshape | solution.py:159
  117.3 0.9 fusion.15
  (56 shorter events, 11.0 us)
Async XLA Ops:
  9.7 2.2 %copy-start.1 = (s32[1,128]{1,0:T(1,128)S(1)}, s32[1,128]{1,0:T(1,128)}, u32[]{:S(2)}) copy-start(s32[1,128]{1,0:T(1,128)} %param.12) | copy-start | bytes 1540
  17.2 1.0 copy-start
  26.8 16.2 %all-to-all-start = ((f32[256,1,2,128]{3,2,1,0:T(2,128)}), f32[256,1,2,128]{3,2,1,0:T(2,128)S(1)}, u32[]{:S(2)}, u32[]{:S(2)}) async-start(f32[256,1,2,128]{3,2,1,0:T(2,128)} %copy.95), calls=%async_computation | async-start | bytes 524288 | tf_op jit(solution)/shard_map/all_to_all | solution.py:134
  43.2 1.4 %collective-permute-start = (f32[16,16,128]{2,1,0:T(8,128)S(1)}, f32[16,16,128]{2,1,0:T(8,128)S(1)}, u32[]{:S(2)}, u32[]{:S(2)}) collective-permute-start(f32[16,16,128]{2,1,0:T(8,128)S(1)} %bitcast.145), channel_id=1, source_target_pairs={{0,8},{8,0},{16,24},{24,16},{1,9},{9,1},{17,25},{25,17},{2,10},{10... | collective-permute-start | bytes 393224 | tf_op jit(solution)/shard_map/ppermute | solution.py:20
  90.7 1.4 %collective-permute-start.1 = (f32[16,16,128]{2,1,0:T(8,128)S(1)}, f32[16,16,128]{2,1,0:T(8,128)S(1)}, u32[]{:S(2)}, u32[]{:S(2)}) collective-permute-start(f32[16,16,128]{2,1,0:T(8,128)S(1)} %get-tuple-element.21), channel_id=1, source_target_pairs={{0,8},{8,0},{16,24},{24,16},{1,9},{9,1},{17,25},{25,17},{2,10},{10... | collective-permute-start | bytes 393224 | tf_op jit(solution)/shard_map/ppermute | solution.py:20
  97.2 12.9 %all-to-all-start.1 = ((f32[8,32,1,2,128]{4,1,3,2,0:T(8,128)}), f32[8,32,1,2,128]{4,1,3,2,0:T(8,128)S(1)}, u32[]{:S(2)}, u32[]{:S(2)}) async-start(f32[8,32,1,2,128]{4,1,3,2,0:T(8,128)} %copy_dynamic-update-slice_fusion), calls=%async_computation.1 | async-start | bytes 524288 | tf_op jit(solution)/shard_map/all_to_all | solution.py:156
